TPU v7x, 128 devices: a whole 4x4x4 slice. The times are simulated.
128 devices in a mesh: section: 4 (over y), dp: 2 (over core), expert: 16 (over x, z).
Axes of the slice: x: 4, y: 4, z: 4, core: 2. Of those that a mesh axis runs over, the one named last changes fastest.
Arguments:
- stashed: bfloat16 [4, 6144, 2048], P('section', ('dp', 'expert')), may hold values from -6 to 6
- expert_ids: int32 [4, 6144, 8], P('section', ('dp', 'expert')), may hold values from 0 to 63, all different within a row; in each aligned block of 192 rows (0 to 191, 192 to 383, ..., all dimensions but the last counted through in order) at most 48 rows name the same one
- route_probs: float32 [4, 6144, 8], P('section', ('dp', 'expert')), may hold values from 0.02 to 1
- w_gate: bfloat16 [4, 64, 2048, 768], P('section', ('dp', 'expert')), may hold values from -0.125 to 0.125
- w_up: bfloat16 [4, 64, 2048, 768], P('section', ('dp', 'expert')), may hold values from -0.125 to 0.125
- w_down: bfloat16 [4, 64, 768, 2048], P('section', ('dp', 'expert')), may hold values from -0.21875 to 0.21875
Outputs:
- handed: bfloat16 [4, 6144, 2048], P('section', ('dp', 'expert'))
- balance: float32 [4], P('section')
Inputs may be any that keep to these rules, and one draw needn't show every extreme that they name: `expert_ids`: each token names 8 different experts; among the tokens of one device (aligned blocks of 192 tokens) no expert is named more than 48 times, and in every draw some expert is named exactly 48 times in some block.
All inputs are finite; a program needn't handle non-finite values.
Results may differ from a plain program's by a relative error of at most 0.0032.
Values may be sent and summed in bfloat16 or wider, within the bound.
No kernel may reach another device: no remote copies, remote signals or barrier semaphores. Data moves between devices by JAX's collectives and lax.ppermute only.
A program may use at most 128 MiB of HBM per device.

v0:
```python
import jax
import jax.numpy as jnp
from jax import lax
from jax.sharding import PartitionSpec as P


def passed_along(value, axis, steps):
    count = lax.axis_size(axis)
    pairs = [(source, (source + steps) % count) for source in range(count)]
    return lax.ppermute(value, axis, pairs)


def expert_rows(received, gate_w, up_w, down_w, form_in, form_out):
    gate_act = jnp.einsum(form_in, received, gate_w, preferred_element_type=jnp.float32)
    up_act = jnp.einsum(form_in, received, up_w, preferred_element_type=jnp.float32)
    hidden = (jax.nn.silu(gate_act) * up_act).astype(jnp.bfloat16)
    return jnp.einsum(form_out, hidden, down_w, preferred_element_type=jnp.float32).astype(
        jnp.bfloat16
    )


def per_device(stashed, expert_ids, route_probs, w_gate, w_up, w_down):
    tokens_in = stashed[0]
    choice_ids = expert_ids[0]
    probs = route_probs[0]
    gate_w = w_gate[0]
    up_w = w_up[0]
    down_w = w_down[0]
    expert_count = lax.axis_size("expert")
    dp_count = lax.axis_size("dp")
    local_count = gate_w.shape[0]
    all_experts = dp_count * expert_count * local_count
    token_count, top_count = choice_ids.shape
    model_width = tokens_in.shape[1]
    capacity = 2 * token_count * top_count // all_experts
    inputs = tokens_in.astype(jnp.float32)
    normed = (inputs * lax.rsqrt(jnp.mean(inputs * inputs, axis=-1, keepdims=True) + 1e-06)).astype(
        jnp.bfloat16
    )
    flat_ids = choice_ids.reshape(-1)
    labels = jnp.arange(all_experts, dtype=jnp.int32)
    onehot = (flat_ids[:, None] == labels[None, :]).astype(jnp.int32)
    running = jnp.cumsum(onehot, axis=0)
    position = jnp.sum(running * onehot, axis=1) - 1
    slot_rows = flat_ids * capacity + position
    sent_rows = (
        jnp.zeros((all_experts * capacity, model_width), jnp.bfloat16)
        .at[slot_rows]
        .set(jnp.repeat(normed, top_count, axis=0))
    )
    arranged = sent_rows.reshape(dp_count * expert_count, local_count, capacity, model_width)
    received = lax.all_to_all(arranged, ("dp", "expert"), split_axis=0, concat_axis=0, tiled=True)
    result = expert_rows(received, gate_w, up_w, down_w, "secd,edf->secf", "secf,efd->secd")
    returned = lax.all_to_all(result, ("dp", "expert"), split_axis=0, concat_axis=0, tiled=True)
    picked = returned.reshape(all_experts * capacity, model_width)[slot_rows]
    picked = picked.reshape(token_count, top_count, model_width).astype(jnp.float32)
    weights = probs / jnp.sum(probs, axis=-1, keepdims=True)
    mixture = jnp.sum(weights[:, :, None] * picked, axis=1)
    layer_out = (inputs + mixture).astype(jnp.bfloat16)
    counts = jnp.sum(onehot, axis=0).astype(jnp.float32)
    mass = jnp.dot(weights.reshape(-1), onehot.astype(jnp.float32), precision=lax.Precision.HIGHEST)
    counts_all, mass_all = lax.psum((counts, mass), ("dp", "expert"))
    tokens_all = token_count * dp_count * expert_count
    loss = all_experts * jnp.sum(counts_all / (tokens_all * top_count) * (mass_all / tokens_all))
    handed = passed_along(layer_out, "section", 1)
    return (handed[None], loss.reshape(1))


def solution(mesh):
    placed = (
        P("section", ("dp", "expert"), None),
        P("section", ("dp", "expert"), None),
        P("section", ("dp", "expert"), None),
        P("section", ("dp", "expert"), None, None),
        P("section", ("dp", "expert"), None, None),
        P("section", ("dp", "expert"), None, None),
    )
    return jax.shard_map(
        per_device,
        mesh=mesh,
        in_specs=placed,
        out_specs=(P("section", ("dp", "expert"), None), P("section")),
        check_vma=False,
    )
```

profile of v0, /device:TPU:2, one launch (start us, length us, event | category | flops | bytes accessed | tf_op | source)
XLA Modules:
  0.0 558.4 jit_solution(3848793365307210415)
XLA Ops:
  0.6 0.8 copy.21
  1.4 0.1 eq.29
  1.5 0.1 eq.25
  1.7 0.7 broadcast_multiply_fusion
  2.4 18.1 %reduce-window.6 = s32[64,12,128]{2,1,0:T(8,128)S(1)} reduce-window(s32[64,12,128]{2,1,0:T(8,128)S(1)} %fusion.29, s32[]{:T(128)} %constant.9.clone.1), window={size=1x1x128 pad=0_0x0_0x127_0}, to_apply=%region_1.0 | reduce-window | flops 12484608 | bytes 786436 | tf_op jit(solution)/shard_map/reduce-window
  20.5 0.2 slice.10
  20.7 0.3 copy.23
  21.0 0.1 copy.24
  21.1 0.2 broadcast_add_fusion
  21.3 0.2 convert_reduce_fusion
  21.6 0.1 copy.20
  21.7 0.1 mul.51
  21.8 1.4 fusion.26
  23.2 1.3 fusion.27
  24.5 16.3 %scatter_custom_fusion = bf16[3072,2048]{1,0:T(8,128)(2,1)} fusion(s32[1536]{0:T(1024)S(1)} %fusion.33, bf16[]{:T(256)} %constant.8.clone.1, bf16[192,2048]{1,0:T(8,128)(2,1)S(1)} %fusion.27), kind=kCustom, calls=%fused_computation.19 | custom fusion | bytes 13369346 | tf_op jit(solution)/shard_map/scatter | solution.py:49
  40.9 149.1 %all_to_all.10 = bf16[32,2,48,2048]{3,2,1,0:T(8,128)(2,1)S(1)} all-to-all(bf16[32,2,48,2048]{3,2,1,0:T(8,128)(2,1)} %bitcast.78), channel_id=1, replica_groups=mesh['section'=4,'dp'=2,'expert'=16] {'dp','expert'}, dimensions={0} | all-to-all | bytes 25165824 | tf_op jit(solution)/shard_map/all_to_all | solution.py:52
  189.9 0.0 copy-start
  189.9 4.5 copy-done
  194.4 14.1 %fusion.1 = f32[2,32,48,768]{3,2,1,0:T(8,128)} fusion(bf16[32,2,48,2048]{3,2,1,0:T(8,128)(2,1)S(1)} %all_to_all.10, bf16[1,2,2048,768]{3,2,1,0:T(8,128)(2,1)} %param.10), kind=kOutput, calls=%fused_computation.5 | convolution fusion | flops 9663676416 | bytes 28311552 | tf_op jit(solution)/shard_map/secd,edf->secf/dot_general | solution.py:15
  208.4 29.3 %convert_bitcast_fusion = bf16[32,2,48,2048]{3,2,0,1:T(8,128)(2,1)} fusion(bf16[1,2,768,2048]{3,2,1,0:T(8,128)(2,1)} %param.11, f32[2,32,48,768]{3,2,1,0:T(8,128)} %fusion.1, bf16[32,2,48,2048]{3,2,1,0:T(8,128)(2,1)} %copy-done, bf16[1,2,2048,768]{3,2,1,0:T(8,128)(2,1)} %param.9), kind=kOutput, calls=%fused_computation.4 | convolution fusion | flops 19347800064 | bytes 47185920 | tf_op jit(solution)/shard_map/secf,efd->secd/dot_general | solution.py:17
  237.8 10.8 %copy.27 = bf16[32,2,48,2048]{3,2,1,0:T(8,128)(2,1)} copy(bf16[32,2,48,2048]{3,2,0,1:T(8,128)(2,1)} %convert_bitcast_fusion) | data formatting | bytes 25165824 | tf_op jit(solution)/shard_map/convert_element_type | solution.py:17
  248.6 0.0 copy-start.2
  248.6 5.4 all-to-all-start.1
  254.0 0.0 copy-done.2
  254.1 0.1 copy.19
  254.2 194.4 %all-to-all-done.1 = bf16[32,2,48,2048]{3,2,1,0:T(8,128)(2,1)} async-done(((bf16[32,2,48,2048]{3,2,1,0:T(8,128)(2,1)}), bf16[32,2,48,2048]{3,2,1,0:T(8,128)(2,1)}, u32[]{:S(2)}, u32[]{:S(2)}) %all-to-all-start.1) | async-done | bytes 12582944 | tf_op jit(solution)/shard_map/all_to_all | solution.py:54
  448.6 0.0 copy-start.1
  448.6 19.0 %gather_fusion = bf16[1536,2048]{1,0:T(8,128)(2,1)} fusion(bf16[3072,2048]{1,0:T(8,128)(2,1)} %bitcast.19, s32[2048]{0:T(1024)S(1)} %pad_clamp_fusion), kind=kCustom, calls=%fused_computation | custom fusion | bytes 12589056 | tf_op jit(solution)/shard_map/gather | solution.py:55
  467.6 9.2 %fusion = f32[192,2048]{1,0:T(8,128)S(1)} fusion(bf16[1536,2048]{1,0:T(8,128)(2,1)} %gather_fusion, f32[192,8]{1,0:T(8,128)S(1)} %copy.19), kind=kLoop, calls=%fused_computation.3 | loop fusion | flops 9043968 | bytes 7870464 | tf_op jit(solution)/shard_map/reduce_sum | solution.py:58
  476.9 0.0 copy-done.1
  476.9 0.2 fusion.28
  477.1 1.7 collective-permute-start
  478.7 0.1 copy.28
  478.9 0.1 div.39.clone
  478.9 0.1 div.46
  479.1 0.1 squeeze.19
  479.2 0.4 convolution_bitcast_fusion
  479.6 75.5 %all-reduce = (f32[64]{0:T(128)S(1)}, f32[64]{0:T(128)S(1)}) all-reduce(f32[64]{0:T(128)S(1)} %convolution_bitcast_fusion, f32[64]{0:T(128)S(1)} %convert_element_type.51), channel_id=1, replica_groups=mesh['section'=4,'dp'=2,'expert'=16] {'dp','expert'}, use_global_device_ids=true, to_apply=%region_9.10 | all-reduce | flops 128 | bytes 1024 | tf_op jit(solution)/shard_map/psum | solution.py:62
  555.1 0.6 multiply_reduce_fusion
  556.4 0.0 collective-permute-done
  556.4 0.9 copy.44
  (11 shorter events, 0.2 us)
Async XLA Ops:
  189.9 4.5 copy-start
  248.6 5.5 copy-start.2
  248.6 200.0 %all-to-all-start.1 = ((bf16[32,2,48,2048]{3,2,1,0:T(8,128)(2,1)}), bf16[32,2,48,2048]{3,2,1,0:T(8,128)(2,1)}, u32[]{:S(2)}, u32[]{:S(2)}) async-start(bf16[32,2,48,2048]{3,2,1,0:T(8,128)(2,1)} %copy.27), calls=%async_computation.1 | async-start | bytes 25165824 | tf_op jit(solution)/shard_map/all_to_all | solution.py:54
  448.6 28.2 %copy-start.1 = (bf16[1,192,2048]{2,1,0:T(8,128)(2,1)S(1)}, bf16[1,192,2048]{2,1,0:T(8,128)(2,1)}, u32[]{:S(2)}) copy-start(bf16[1,192,2048]{2,1,0:T(8,128)(2,1)} %param.6) | copy-start | bytes 2359300
  477.1 79.3 %collective-permute-start = (bf16[192,2048]{1,0:T(8,128)(2,1)S(1)}, bf16[192,2048]{1,0:T(8,128)(2,1)S(1)}, u32[]{:S(2)}, u32[]{:S(2)}) collective-permute-start(bf16[192,2048]{1,0:T(8,128)(2,1)S(1)} %fusion.28), channel_id=1, source_target_pairs={{0,32},{32,64},{64,96},{96,0},{1,33},{33,65},{65,97},{97,1},{2,34}... | collective-permute-start | bytes 2359304 | tf_op jit(solution)/shard_map/ppermute | solution.py:10
where the time goes:
time: 559 us; the launch traced here: 558 us
  blocking collectives  225 us (40%)
  waiting for transfers between devices  194 us (35%)
  local copies, waits for them, and re-layouts  53.8 us (10%)
  matrix products  43.8 us (8%)
  other arithmetic  32.1 us (6%)
  starting transfers between devices  7.09 us (1%)
    all_to_all x1, waiting for transfers between devices, per_device(): lax.all_to_all(result, ('dp', 'expert'), split_axis=0, concat_axis=0, til...  194 us
    all_to_all x1, blocking collectives, per_device(): lax.all_to_all(arranged, ('dp', 'expert'), split_axis=0, concat_axis=0, t...  149 us
    psum x1, blocking collectives, per_device(): counts_all, mass_all = lax.psum((counts, mass), ('dp', 'expert'))  75.5 us
    dot_general x1, matrix products, expert_rows(): jnp.einsum(form_out, hidden, down_w, preferred_element_type=jnp.float32)  29.3 us
    gather x1, local copies, waits for them, and re-layouts, per_device(): picked = returned.reshape(all_experts * capacity, model_width)[slot_rows]  19 us
    another operation x3, other arithmetic  18.4 us
    scatter x1, local copies, waits for them, and re-layouts, per_device(): sent_rows = jnp.zeros((all_experts * capacity, model_width), jnp.bfloat16...  16.3 us
    dot_general x1, matrix products, expert_rows(): jnp.einsum(form_in, received, up_w, preferred_element_type=jnp.float32)  14.1 us
  transfers between devices with their start and end apart: 2, of which 1 were waited for; matrix products, arithmetic and copies ran while one was open for 0% of the time, Pallas kernels for 0%

commit v1 on v0

--- a/solution.py
+++ b/solution.py
@@ -59,7 +59,7 @@
     layer_out = (inputs + mixture).astype(jnp.bfloat16)
     counts = jnp.sum(onehot, axis=0).astype(jnp.float32)
     mass = jnp.dot(weights.reshape(-1), onehot.astype(jnp.float32), precision=lax.Precision.HIGHEST)
-    counts_all, mass_all = lax.psum((counts, mass), ("dp", "expert"))
+    counts_all, mass_all = lax.psum(lax.psum((counts, mass), "dp"), "expert")
     tokens_all = token_count * dp_count * expert_count
     loss = all_experts * jnp.sum(counts_all / (tokens_all * top_count) * (mass_all / tokens_all))
     handed = passed_along(layer_out, "section", 1)

time: 559 us -> 533 us (0.953)
  blocking collectives: 225 us -> 198 us
    psum x1 -> x2, blocking collectives: 75.5 us -> 48.6 us  [per_device(): counts_all, mass_all = lax.psum(lax.psum((counts, mass), 'dp'), 'expert')]
where the time goes in v1:
time: 533 us; the launch traced here: 531 us
  blocking collectives  198 us (37%)
  waiting for transfers between devices  194 us (36%)
  local copies, waits for them, and re-layouts  53.8 us (10%)
  matrix products  43.8 us (8%)
  other arithmetic  32.1 us (6%)
  starting transfers between devices  7.09 us (1%)
    all_to_all x1, waiting for transfers between devices, per_device(): lax.all_to_all(result, ('dp', 'expert'), split_axis=0, concat_axis=0, til...  194 us
    all_to_all x1, blocking collectives, per_device(): lax.all_to_all(arranged, ('dp', 'expert'), split_axis=0, concat_axis=0, t...  149 us
    psum x2, blocking collectives, per_device(): counts_all, mass_all = lax.psum(lax.psum((counts, mass), 'dp'), 'expert')  48.6 us
    dot_general x1, matrix products, expert_rows(): jnp.einsum(form_out, hidden, down_w, preferred_element_type=jnp.float32)  29.3 us
    gather x1, local copies, waits for them, and re-layouts, per_device(): picked = returned.reshape(all_experts * capacity, model_width)[slot_rows]  19 us
    another operation x3, other arithmetic  18.4 us
    scatter x1, local copies, waits for them, and re-layouts, per_device(): sent_rows = jnp.zeros((all_experts * capacity, model_width), jnp.bfloat16...  16.3 us
    dot_general x1, matrix products, expert_rows(): jnp.einsum(form_in, received, up_w, preferred_element_type=jnp.float32)  14.1 us
  transfers between devices with their start and end apart: 2, of which 1 were waited for; matrix products, arithmetic and copies ran while one was open for 0% of the time, Pallas kernels for 0%

profile of v1, /device:TPU:2, one launch (start us, length us, event | category | flops | bytes accessed | tf_op | source)
XLA Modules:
  0.0 531.5 jit_solution(830386422751429436)
XLA Ops:
  0.6 0.8 copy.21
  1.4 0.1 eq.29
  1.5 0.1 eq.25
  1.7 0.7 broadcast_multiply_fusion
  2.4 18.1 %reduce-window.6 = s32[64,12,128]{2,1,0:T(8,128)S(1)} reduce-window(s32[64,12,128]{2,1,0:T(8,128)S(1)} %fusion.29, s32[]{:T(128)} %constant.9.clone.1), window={size=1x1x128 pad=0_0x0_0x127_0}, to_apply=%region_1.0 | reduce-window | flops 12484608 | bytes 786436 | tf_op jit(solution)/shard_map/reduce-window
  20.5 0.2 slice.10
  20.7 0.3 copy.23
  21.0 0.1 copy.24
  21.1 0.2 broadcast_add_fusion
  21.3 0.2 convert_reduce_fusion
  21.6 0.1 copy.20
  21.7 0.1 mul.51
  21.8 1.4 fusion.26
  23.2 1.3 fusion.27
  24.5 16.3 %scatter_custom_fusion = bf16[3072,2048]{1,0:T(8,128)(2,1)} fusion(s32[1536]{0:T(1024)S(1)} %fusion.33, bf16[]{:T(256)} %constant.8.clone.1, bf16[192,2048]{1,0:T(8,128)(2,1)S(1)} %fusion.27), kind=kCustom, calls=%fused_computation.19 | custom fusion | bytes 13369346 | tf_op jit(solution)/shard_map/scatter | solution.py:49
  40.9 149.1 %all_to_all.10 = bf16[32,2,48,2048]{3,2,1,0:T(8,128)(2,1)S(1)} all-to-all(bf16[32,2,48,2048]{3,2,1,0:T(8,128)(2,1)} %bitcast.78), channel_id=1, replica_groups=mesh['section'=4,'dp'=2,'expert'=16] {'dp','expert'}, dimensions={0} | all-to-all | bytes 25165824 | tf_op jit(solution)/shard_map/all_to_all | solution.py:52
  189.9 0.0 copy-start
  189.9 4.5 copy-done
  194.4 14.1 %fusion.1 = f32[2,32,48,768]{3,2,1,0:T(8,128)} fusion(bf16[32,2,48,2048]{3,2,1,0:T(8,128)(2,1)S(1)} %all_to_all.10, bf16[1,2,2048,768]{3,2,1,0:T(8,128)(2,1)} %param.10), kind=kOutput, calls=%fused_computation.5 | convolution fusion | flops 9663676416 | bytes 28311552 | tf_op jit(solution)/shard_map/secd,edf->secf/dot_general | solution.py:15
  208.4 29.3 %convert_bitcast_fusion = bf16[32,2,48,2048]{3,2,0,1:T(8,128)(2,1)} fusion(bf16[1,2,768,2048]{3,2,1,0:T(8,128)(2,1)} %param.11, f32[2,32,48,768]{3,2,1,0:T(8,128)} %fusion.1, bf16[32,2,48,2048]{3,2,1,0:T(8,128)(2,1)} %copy-done, bf16[1,2,2048,768]{3,2,1,0:T(8,128)(2,1)} %param.9), kind=kOutput, calls=%fused_computation.4 | convolution fusion | flops 19347800064 | bytes 47185920 | tf_op jit(solution)/shard_map/secf,efd->secd/dot_general | solution.py:17
  237.8 10.8 %copy.27 = bf16[32,2,48,2048]{3,2,1,0:T(8,128)(2,1)} copy(bf16[32,2,48,2048]{3,2,0,1:T(8,128)(2,1)} %convert_bitcast_fusion) | data formatting | bytes 25165824 | tf_op jit(solution)/shard_map/convert_element_type | solution.py:17
  248.6 0.0 copy-start.2
  248.6 5.4 %all-to-all-start.1 = ((bf16[32,2,48,2048]{3,2,1,0:T(8,128)(2,1)}), bf16[32,2,48,2048]{3,2,1,0:T(8,128)(2,1)}, u32[]{:S(2)}, u32[]{:S(2)}) async-start(bf16[32,2,48,2048]{3,2,1,0:T(8,128)(2,1)} %copy.27), calls=%async_computation.1 | async-start | bytes 25165824 | tf_op jit(solution)/shard_map/all_to_all | solution.py:54
  254.0 0.0 copy-done.2
  254.1 0.1 copy.19
  254.2 194.4 %all-to-all-done.1 = bf16[32,2,48,2048]{3,2,1,0:T(8,128)(2,1)} async-done(((bf16[32,2,48,2048]{3,2,1,0:T(8,128)(2,1)}), bf16[32,2,48,2048]{3,2,1,0:T(8,128)(2,1)}, u32[]{:S(2)}, u32[]{:S(2)}) %all-to-all-start.1) | async-done | bytes 12582944 | tf_op jit(solution)/shard_map/all_to_all | solution.py:54
  448.6 0.0 copy-start.1
  448.6 19.0 %gather_fusion = bf16[1536,2048]{1,0:T(8,128)(2,1)} fusion(bf16[3072,2048]{1,0:T(8,128)(2,1)} %bitcast.19, s32[2048]{0:T(1024)S(1)} %pad_clamp_fusion), kind=kCustom, calls=%fused_computation | custom fusion | bytes 12589056 | tf_op jit(solution)/shard_map/gather | solution.py:55
  467.6 9.2 %fusion = f32[192,2048]{1,0:T(8,128)S(1)} fusion(bf16[1536,2048]{1,0:T(8,128)(2,1)} %gather_fusion, f32[192,8]{1,0:T(8,128)S(1)} %copy.19), kind=kLoop, calls=%fused_computation.3 | loop fusion | flops 9043968 | bytes 7870464 | tf_op jit(solution)/shard_map/reduce_sum | solution.py:58
  476.9 0.0 copy-done.1
  476.9 0.2 fusion.28
  477.1 1.7 collective-permute-start
  478.7 0.1 copy.28
  478.9 0.1 div.39.clone
  478.9 0.1 div.46
  479.1 0.1 squeeze.19
  479.2 0.4 convolution_bitcast_fusion
  479.6 2.5 all-reduce.1
  482.1 46.1 %all-reduce = (f32[64]{0:T(128)S(1)}, f32[64]{0:T(128)S(1)}) all-reduce(f32[64]{0:T(128)S(1)} %get-tuple-element.6, f32[64]{0:T(128)S(1)} %get-tuple-element.7), channel_id=1, replica_groups=mesh['section'=4,'dp'=2,'expert'=16] {'expert'}, use_global_device_ids=true, to_apply=%region_11.12 | all-reduce | flops 128 | bytes 1024 | tf_op jit(solution)/shard_map/psum | solution.py:62
  528.2 0.6 multiply_reduce_fusion
  529.5 0.0 collective-permute-done
  529.5 0.9 copy.44
  (11 shorter events, 0.2 us)
Async XLA Ops:
  189.9 4.5 copy-start
  248.6 5.5 %copy-start.2 = (f32[1,192,8]{1,2,0:T(8,128)S(1)}, f32[1,192,8]{1,2,0:T(8,128)}, u32[]{:S(2)}) copy-start(f32[1,192,8]{1,2,0:T(8,128)} %param.8) | copy-start | bytes 18436
  248.6 200.0 %all-to-all-start.1 = ((bf16[32,2,48,2048]{3,2,1,0:T(8,128)(2,1)}), bf16[32,2,48,2048]{3,2,1,0:T(8,128)(2,1)}, u32[]{:S(2)}, u32[]{:S(2)}) async-start(bf16[32,2,48,2048]{3,2,1,0:T(8,128)(2,1)} %copy.27), calls=%async_computation.1 | async-start | bytes 25165824 | tf_op jit(solution)/shard_map/all_to_all | solution.py:54
  448.6 28.2 %copy-start.1 = (bf16[1,192,2048]{2,1,0:T(8,128)(2,1)S(1)}, bf16[1,192,2048]{2,1,0:T(8,128)(2,1)}, u32[]{:S(2)}) copy-start(bf16[1,192,2048]{2,1,0:T(8,128)(2,1)} %param.6) | copy-start | bytes 2359300
  477.1 52.4 %collective-permute-start = (bf16[192,2048]{1,0:T(8,128)(2,1)S(1)}, bf16[192,2048]{1,0:T(8,128)(2,1)S(1)}, u32[]{:S(2)}, u32[]{:S(2)}) collective-permute-start(bf16[192,2048]{1,0:T(8,128)(2,1)S(1)} %fusion.28), channel_id=1, source_target_pairs={{0,32},{32,64},{64,96},{96,0},{1,33},{33,65},{65,97},{97,1},{2,34}... | collective-permute-start | bytes 2359304 | tf_op jit(solution)/shard_map/ppermute | solution.py:10
